TPU v7x, 32 devices: a whole 2x2x4 slice. The times are simulated.
32 devices in a mesh: dp: 4 (over y, x), tm: 4 (over z), rows: 2 (over core).
Axes of the slice: x: 2, y: 2, z: 4, core: 2. Of those that a mesh axis runs over, the one named last changes fastest.
Arguments:
- latents: bfloat16 [4, 8, 8, 32, 384], P('dp', 'tm', 'rows'), may hold values from -6 to 6
- hidden: bfloat16 [4, 8, 8, 32, 384], P('dp', 'tm', 'rows'), may hold values from -8 to 8
- cotangent: bfloat16 [4, 8, 8, 32, 384], P('dp', 'tm', 'rows'), may hold values from -6 to 6
- conv_one: bfloat16 [3, 3, 3, 384, 384], replicated, may hold values from -0.0625 to 0.0625
- conv_two: bfloat16 [3, 3, 3, 384, 384], replicated, may hold values from -0.0625 to 0.0625
- lengths: int32 [4], P('dp'), may hold values from 3 to 8, as said below
Outputs:
- latent_grad: float32 [4, 8, 8, 32, 384], P('dp', None, None, ('tm', 'rows'))
Inputs may be any that keep to these rules, and one draw needn't show every extreme that they name: `lengths`: at least one clip has all 8 frames valid.
All inputs are finite; a program needn't handle non-finite values.
Results may differ from a plain program's by a relative error of at most 0.00092.
Values may be sent and summed in bfloat16 or wider, within the bound.
No kernel may reach another device: no remote copies, remote signals or barrier semaphores. Data moves between devices by JAX's collectives and lax.ppermute only.
A program may use at most 64 MiB of HBM per device.

v0:
```python
import jax
import jax.numpy as jnp
from jax import lax
from jax.sharding import PartitionSpec as P


def with_halo(block, sides, width):
    for axis, dim in sides:
        count = lax.axis_size(axis)
        forward = [(i, i + 1) for i in range(count - 1)]
        backward = [(target, source) for source, target in forward]
        low = lax.ppermute(
            lax.slice_in_dim(block, block.shape[dim] - width, None, axis=dim), axis, forward
        )
        high = lax.ppermute(lax.slice_in_dim(block, 0, width, axis=dim), axis, backward)
        block = jnp.concatenate([low, block, high], axis=dim)
    return block


def shifted(value, axis, by):
    devices = lax.axis_size(axis)
    pairs = [(i, i + by) for i in range(devices) if 0 <= i + by < devices]
    return lax.ppermute(value, axis, pairs)


def silu_slope(values):
    sigmoid_of = jax.nn.sigmoid(values)
    return sigmoid_of * (1.0 + values * (1.0 - sigmoid_of))


def extended(row_band, next_frames):
    joined = jnp.concatenate([row_band, next_frames], axis=0)
    return jnp.pad(joined, ((0, 0), (0, 0), (1, 1), (0, 0)))


def transposed_conv(padded, kernel, frame_count, row_count, col_count):
    summed = jnp.zeros((frame_count, row_count, col_count, kernel.shape[4]), jnp.float32)
    for time_tap in range(3):
        for row_tap in range(3):
            slab_rows = padded[time_tap : time_tap + frame_count, row_tap : row_tap + row_count]
            stacked = jnp.stack(
                [slab_rows[:, :, col_tap : col_tap + col_count] for col_tap in range(3)], axis=3
            )
            kernel_slice = kernel[2 - time_tap, 2 - row_tap, ::-1]
            summed = summed + jnp.einsum(
                "frwkc,kdc->frwd", stacked, kernel_slice, preferred_element_type=jnp.float32
            )
    return summed


def on_device(latents, hidden, cotangent, conv_one, conv_two, lengths):
    frame_dev = latents.shape[1]
    row_dev = latents.shape[2]
    col_count = latents.shape[3]
    channels = latents.shape[4]
    first_frame = lax.axis_index("tm") * frame_dev
    frames = first_frame + jnp.arange(frame_dev, dtype=jnp.int32)
    live_frames = frames < lengths[0]
    masked = jnp.where(live_frames[:, None, None, None], cotangent[0], jnp.zeros_like(cotangent[0]))
    cot_band = with_halo(masked, (("rows", 1),), 1)
    cot_next = shifted(cot_band, "tm", -1)
    grad_act = transposed_conv(
        extended(cot_band, cot_next), conv_two, frame_dev, row_dev, col_count
    )
    grad_hidden = (grad_act * silu_slope(hidden[0].astype(jnp.float32))).astype(jnp.bfloat16)
    hidden_band = with_halo(grad_hidden, (("rows", 1),), 1)
    hidden_next = shifted(hidden_band, "tm", -1)
    grad_input = transposed_conv(
        extended(hidden_band, hidden_next), conv_one, frame_dev, row_dev, col_count
    )
    result = masked.astype(jnp.float32) + grad_input * silu_slope(latents[0].astype(jnp.float32))
    result = result[None]
    time_devs = lax.axis_size("tm")
    row_devs = lax.axis_size("rows")
    arrived = lax.all_to_all(
        result[:, None], ("tm", "rows"), split_axis=4, concat_axis=1, tiled=True
    )
    col_dev = arrived.shape[4]
    arranged = arrived.reshape(1, time_devs, row_devs, frame_dev, row_dev, col_dev, channels)
    arranged = arranged.transpose(0, 1, 3, 2, 4, 5, 6)
    return arranged.reshape(1, time_devs * frame_dev, row_devs * row_dev, col_dev, channels)


def solution(mesh):
    in_specs = (
        P("dp", "tm", "rows", None, None),
        P("dp", "tm", "rows", None, None),
        P("dp", "tm", "rows", None, None),
        P(),
        P(),
        P("dp"),
    )
    out_specs = P("dp", None, None, ("tm", "rows"), None)
    return jax.shard_map(
        on_device, mesh=mesh, in_specs=in_specs, out_specs=out_specs, check_vma=False
    )
```

profile of v0, /device:TPU:0, one launch (start us, length us, event | category | flops | bytes accessed | tf_op | source)
XLA Modules:
  0.0 96.8 jit_solution(17803353701645760821)
XLA Ops:
  0.7 1.0 %bitcast_select_fusion.1 = bf16[2,4,32,384]{3,2,1,0:T(8,128)(2,1)S(1)} fusion(bf16[1,2,4,32,384]{4,3,2,1,0:T(8,128)(2,1)} %param.8, pred[2]{0:T(512)(128)(4,1)S(1)} %add_compare_fusion), kind=kLoop, calls=%fused_computation.207 | loop fusion | flops 98304 | bytes 393218 | tf_op jit(solution)/shard_map/jit(_where)/select_n | solution.py:59
  1.7 2.4 %collective-permute-start = (bf16[2,1,32,384]{3,2,1,0:T(8,128)(2,1)S(1)}, bf16[2,1,32,384]{3,2,1,0:T(8,128)(2,1)S(1)}, u32[]{:S(2)}, u32[]{:S(2)}) collective-permute-start(bf16[2,1,32,384]{3,2,1,0:T(8,128)(2,1)S(1)} %get-tuple-element.77), channel_id=1, source_target_pairs={{0,1},{2,3},{4,5},{6,7},{8,9},{10,11},{12,13},{14,15},{16,17},{18,... | collective-permute-start | bytes 147464 | tf_op jit(solution)/shard_map/ppermute | solution.py:12
  4.1 1.3 %collective-permute-start.1 = (bf16[2,1,32,384]{3,2,1,0:T(8,128)(2,1)S(1)}, bf16[2,1,32,384]{3,2,1,0:T(8,128)(2,1)S(1)}, u32[]{:S(2)}, u32[]{:S(2)}) collective-permute-start(bf16[2,1,32,384]{3,2,1,0:T(8,128)(2,1)S(1)} %get-tuple-element.78), channel_id=1, source_target_pairs={{1,0},{3,2},{5,4},{7,6},{9,8},{11,10},{13,12},{15,14},{17,16},{19,... | collective-permute-start | bytes 147464 | tf_op jit(solution)/shard_map/ppermute | solution.py:15
  5.4 5.3 %fusion.122 = (bf16[1,1,3,384,384]{4,3,2,1,0:T(8,128)(2,1)}, bf16[1,1,3,384,384]{4,3,2,1,0:T(8,128)(2,1)S(1)}, bf16[1,1,3,384,384]{4,3,2,1,0:T(8,128)(2,1)S(1)},...) fusion(bf16[3,3,3,384,384]{4,3,2,1,0:T(8,128)(2,1)} %param.10), kind=kLoop, calls=%fused_computation.211 | loop fusion | bytes 15925248 | tf_op jit(solution)/shard_map/slice | solution.py:44
  10.7 2.2 %rev.55 = bf16[1,1,3,384,384]{4,3,2,1,0:T(8,128)(2,1)} reverse(bf16[1,1,3,384,384]{4,3,2,1,0:T(8,128)(2,1)} %get-tuple-element.14), dimensions={2} | reverse | bytes 1769472 | tf_op jit(solution)/shard_map/rev | solution.py:44
  12.9 2.2 %rev.56 = bf16[1,1,3,384,384]{4,3,2,1,0:T(8,128)(2,1)} reverse(bf16[1,1,3,384,384]{4,3,2,1,0:T(8,128)(2,1)} %get-tuple-element.19), dimensions={2} | reverse | bytes 1769472 | tf_op jit(solution)/shard_map/rev | solution.py:44
  15.1 2.2 %rev.57 = bf16[1,1,3,384,384]{4,3,2,1,0:T(8,128)(2,1)} reverse(bf16[1,1,3,384,384]{4,3,2,1,0:T(8,128)(2,1)} %get-tuple-element.18), dimensions={2} | reverse | bytes 1769472 | tf_op jit(solution)/shard_map/rev | solution.py:44
  17.3 2.2 %rev.58 = bf16[1,1,3,384,384]{4,3,2,1,0:T(8,128)(2,1)} reverse(bf16[1,1,3,384,384]{4,3,2,1,0:T(8,128)(2,1)} %get-tuple-element.17), dimensions={2} | reverse | bytes 1769472 | tf_op jit(solution)/shard_map/rev | solution.py:44
  19.5 1.0 %rev.59 = bf16[1,1,3,384,384]{4,3,2,1,0:T(8,128)(2,1)} reverse(bf16[1,1,3,384,384]{4,3,2,1,0:T(8,128)(2,1)S(1)} %get-tuple-element.16), dimensions={2} | reverse | bytes 1769472 | tf_op jit(solution)/shard_map/rev | solution.py:44
  20.5 0.1 rev.60
  20.6 0.1 rev.61
  20.7 1.3 %rev.62 = bf16[1,1,3,384,384]{4,3,2,1,0:T(8,128)(2,1)S(1)} reverse(bf16[1,1,3,384,384]{4,3,2,1,0:T(8,128)(2,1)} %get-tuple-element.21), dimensions={2} | reverse | bytes 1769472 | tf_op jit(solution)/shard_map/rev | solution.py:44
  22.0 2.2 %rev.54 = bf16[1,1,3,384,384]{4,3,2,1,0:T(8,128)(2,1)} reverse(bf16[1,1,3,384,384]{4,3,2,1,0:T(8,128)(2,1)} %get-tuple-element.20), dimensions={2} | reverse | bytes 1769472 | tf_op jit(solution)/shard_map/rev | solution.py:44
  24.2 1.4 %collective-permute-start.2 = (bf16[2,6,32,384]{3,2,1,0:T(8,128)(2,1)S(1)}, bf16[2,6,32,384]{3,2,1,0:T(8,128)(2,1)S(1)}, u32[]{:S(2)}, u32[]{:S(2)}) collective-permute-start(bf16[2,6,32,384]{3,2,1,0:T(8,128)(2,1)S(1)} %pad_maximum_fusion.19), channel_id=1, source_target_pairs={{2,0},{4,2},{6,4},{3,1},{5,3},{7,5},{10,8},{12,10},{14,12},{11,9},... | collective-permute-start | bytes 884744 | tf_op jit(solution)/shard_map/ppermute | solution.py:23
  25.7 0.1 bitcast_select_fusion
  25.8 10.3 %collective-permute-done.2 = bf16[2,6,32,384]{3,2,1,0:T(8,128)(2,1)S(1)} collective-permute-done((bf16[2,6,32,384]{3,2,1,0:T(8,128)(2,1)S(1)}, bf16[2,6,32,384]{3,2,1,0:T(8,128)(2,1)S(1)}, u32[]{:S(2)}, u32[]{:S(2)}) %collective-permute-start.2) | collective-permute-done | bytes 294944 | tf_op jit(solution)/shard_map/ppermute | solution.py:23
  36.1 0.1 pad_maximum_fusion
  36.2 0.7 fusion.82
  36.9 0.2 pad_maximum_fusion.1
  37.1 0.5 fusion.42
  37.6 0.5 fusion.40
  38.1 0.2 pad_maximum_fusion.3
  38.3 0.5 fusion.38
  38.8 0.5 fusion.36
  39.3 0.1 slice_bitcast_fusion.8
  39.4 0.2 pad_maximum_fusion.5
  39.5 0.5 fusion.34
  40.0 0.5 fusion.32
  40.5 0.2 pad_maximum_fusion.7
  40.7 0.5 fusion.30
  41.2 0.5 fusion.28
  41.7 0.7 fusion.9
  42.4 2.2 %collective-permute-start.3 = (bf16[2,1,32,384]{3,2,1,0:T(8,128)(2,1)S(1)}, bf16[2,1,32,384]{3,2,1,0:T(8,128)(2,1)S(1)}, u32[]{:S(2)}, u32[]{:S(2)}) collective-permute-start(bf16[2,1,32,384]{3,2,1,0:T(8,128)(2,1)S(1)} %get-tuple-element.73), channel_id=1, source_target_pairs={{0,1},{2,3},{4,5},{6,7},{8,9},{10,11},{12,13},{14,15},{16,17},{18,... | collective-permute-start | bytes 147464 | tf_op jit(solution)/shard_map/ppermute | solution.py:12
  44.6 1.3 %collective-permute-start.4 = (bf16[2,1,32,384]{3,2,1,0:T(8,128)(2,1)S(1)}, bf16[2,1,32,384]{3,2,1,0:T(8,128)(2,1)S(1)}, u32[]{:S(2)}, u32[]{:S(2)}) collective-permute-start(bf16[2,1,32,384]{3,2,1,0:T(8,128)(2,1)S(1)} %get-tuple-element.74), channel_id=1, source_target_pairs={{1,0},{3,2},{5,4},{7,6},{9,8},{11,10},{13,12},{15,14},{17,16},{19,... | collective-permute-start | bytes 147464 | tf_op jit(solution)/shard_map/ppermute | solution.py:15
  45.9 1.8 %collective-permute-done.4 = bf16[2,1,32,384]{3,2,1,0:T(8,128)(2,1)S(1)} collective-permute-done((bf16[2,1,32,384]{3,2,1,0:T(8,128)(2,1)S(1)}, bf16[2,1,32,384]{3,2,1,0:T(8,128)(2,1)S(1)}, u32[]{:S(2)}, u32[]{:S(2)}) %collective-permute-start.4) | collective-permute-done | bytes 49184 | tf_op jit(solution)/shard_map/ppermute | solution.py:15
  47.7 0.8 pad_maximum_fusion.20
  48.5 1.5 %collective-permute-start.5 = (bf16[2,6,32,384]{3,2,1,0:T(8,128)(2,1)}, bf16[2,6,32,384]{3,2,1,0:T(8,128)(2,1)}, u32[]{:S(2)}, u32[]{:S(2)}) collective-permute-start(bf16[2,6,32,384]{3,2,1,0:T(8,128)(2,1)} %pad_maximum_fusion.20), channel_id=1, source_target_pairs={{2,0},{4,2},{6,4},{3,1},{5,3},{7,5},{10,8},{12,10},{14,12},{11,9},... | collective-permute-start | bytes 884744 | tf_op jit(solution)/shard_map/ppermute | solution.py:23
  50.0 2.7 %fusion.121 = (bf16[1,1,3,384,384]{4,3,2,1,0:T(8,128)(2,1)}, bf16[1,1,3,384,384]{4,3,2,1,0:T(8,128)(2,1)S(1)}, bf16[1,1,3,384,384]{4,3,2,1,0:T(8,128)(2,1)S(1)},...) fusion(bf16[3,3,3,384,384]{4,3,2,1,0:T(8,128)(2,1)S(1)} %bitcas, ...), kind=kLoop, calls=%fused_computation.210 | loop fusion | bytes 15925248 | tf_op jit(solution)/shard_map/slice | solution.py:44
  52.7 2.2 %rev.63 = bf16[1,1,3,384,384]{4,3,2,1,0:T(8,128)(2,1)} reverse(bf16[1,1,3,384,384]{4,3,2,1,0:T(8,128)(2,1)} %get-tuple-element.5), dimensions={2} | reverse | bytes 1769472 | tf_op jit(solution)/shard_map/rev | solution.py:44
  54.9 2.2 %rev.64 = bf16[1,1,3,384,384]{4,3,2,1,0:T(8,128)(2,1)} reverse(bf16[1,1,3,384,384]{4,3,2,1,0:T(8,128)(2,1)} %get-tuple-element.11), dimensions={2} | reverse | bytes 1769472 | tf_op jit(solution)/shard_map/rev | solution.py:44
  57.1 2.2 %rev.65 = bf16[1,1,3,384,384]{4,3,2,1,0:T(8,128)(2,1)} reverse(bf16[1,1,3,384,384]{4,3,2,1,0:T(8,128)(2,1)} %get-tuple-element.10), dimensions={2} | reverse | bytes 1769472 | tf_op jit(solution)/shard_map/rev | solution.py:44
  59.3 2.2 %rev.66 = bf16[1,1,3,384,384]{4,3,2,1,0:T(8,128)(2,1)} reverse(bf16[1,1,3,384,384]{4,3,2,1,0:T(8,128)(2,1)} %get-tuple-element.9), dimensions={2} | reverse | bytes 1769472 | tf_op jit(solution)/shard_map/rev | solution.py:44
  61.4 2.2 %rev.67 = bf16[1,1,3,384,384]{4,3,2,1,0:T(8,128)(2,1)} reverse(bf16[1,1,3,384,384]{4,3,2,1,0:T(8,128)(2,1)} %get-tuple-element.8), dimensions={2} | reverse | bytes 1769472 | tf_op jit(solution)/shard_map/rev | solution.py:44
  63.6 1.0 %rev.68 = bf16[1,1,3,384,384]{4,3,2,1,0:T(8,128)(2,1)} reverse(bf16[1,1,3,384,384]{4,3,2,1,0:T(8,128)(2,1)S(1)} %get-tuple-element.7), dimensions={2} | reverse | bytes 1769472 | tf_op jit(solution)/shard_map/rev | solution.py:44
  64.7 1.0 %rev.69 = bf16[1,1,3,384,384]{4,3,2,1,0:T(8,128)(2,1)} reverse(bf16[1,1,3,384,384]{4,3,2,1,0:T(8,128)(2,1)S(1)} %get-tuple-element.6), dimensions={2} | reverse | bytes 1769472 | tf_op jit(solution)/shard_map/rev | solution.py:44
  65.7 0.1 rev.70
  65.8 0.1 rev.71
  65.9 1.2 %fusion.117 = (bf16[2,4,32,1,384]{4,2,1,0,3:T(8,128)(2,1)S(1)}, bf16[2,4,32,1,384]{4,2,1,0,3:T(8,128)(2,1)S(1)}) fusion(bf16[2,4,32,384]{3,2,1,0:T(8,128)(2,1)} %copy-done.5, bf16[2,1,32,384]{3,2,1,0:T(8,128)(2,1)} %copy-done.16, bf16[2,1,32,384]{3,2,1,0:T(8,128)(2,1)} %copy-done.17), kind=kLoop, calls=%fused_computation.195 | loop fusion | flops 196608 | bytes 688128 | tf_op jit(solution)/shard_map/stack | solution.py:41
  67.1 1.1 %pad_maximum_fusion.9 = bf16[4,6,32,384]{3,2,1,0:T(8,128)(2,1)S(1)} fusion(bf16[2,6,32,384]{3,2,1,0:T(8,128)(2,1)} %collective-permute-done.5, bf16[2,1,32,384]{3,2,1,0:T(8,128)(2,1)} %copy-done.17, bf16[2,4,32,384]{3,2,1,0:T(8,128)(2,1)} %copy-done.5, bf16[2,1,32,384]{3,2,1,0:T(8,128)(2,1)} %copy-done.16), kind=kLoop, calls=%fused_computation.60 | loop fusion | flops 884736 | bytes 1179648 | tf_op jit(solution)/shard_map/concatenate | solution.py:32
  68.2 0.7 fusion.98
  69.0 1.7 %fusion.26 = f32[2,4,32,384,1]{3,2,0,1,4:T(8,128)S(1)} fusion(bf16[1,1,3,384,384]{4,3,2,1,0:T(8,128)(2,1)} %rev.63, bf16[2,4,32,1,384]{4,2,1,0,3:T(8,128)(2,1)S(1)} %get-tuple-element.24, bf16[2,4,32,1,384]{4,2,1,0,3:T(8,128)(2,1)S(1)} %get-tuple-element.71, bf16[2,4,32,1,384]{4,2,1,0,3:T(8,128)(2,1)S(1)} %get-tuple-element.23), kind=kOutput, calls=%fused_computation.27 | convolution fusion | flops 227082240 | bytes 1867776 | tf_op jit(solution)/shard_map/frwkc,kdc->frwd/dot_general | solution.py:45
  70.7 0.5 fusion.24
  71.2 0.5 fusion.22
  71.7 0.5 fusion.20
  72.3 0.5 fusion.18
  72.8 0.5 fusion.16
  73.3 1.2 %slice_bitcast_fusion.2 = (bf16[2,4,32,1,384]{4,2,1,0,3:T(8,128)(2,1)S(1)}, bf16[2,4,32,1,384]{4,2,1,0,3:T(8,128)(2,1)S(1)}, bf16[2,4,32,1,384]{4,2,1,0,3:T(8,128)(2,1)S(1)}) fusion(bf16[2,6,32,384]{3,2,1,0:T(8,128)(2,1)} %collective-permute-done.5), kind=kLoop, calls=%fused_computation.188 | loop fusion | bytes 1179648 | tf_op jit(solution)/shard_map/stack | solution.py:41
  74.5 0.5 fusion.14
  75.0 0.5 fusion.12
  75.5 0.5 fusion.10
  76.0 0.4 fusion.79
  76.4 0.3 copy.46
  76.7 19.3 %all_to_all.15 = f32[1,1,2,4,32,384]{5,3,2,1,0,4:T(4,128)S(1)} all-to-all(f32[1,1,2,4,32,384]{5,3,2,1,0,4:T(4,128)S(1)} %copy.46), channel_id=1, replica_groups=mesh['dp'=4,'tm'=4,'rows'=2] {'tm','rows'}, dimensions={4} | all-to-all | bytes 786432 | tf_op jit(solution)/shard_map/all_to_all | solution.py:75
  96.0 0.8 copy.47
  (56 shorter events, 0.3 us)
Async XLA Ops:
  1.7 22.4 %collective-permute-start = (bf16[2,1,32,384]{3,2,1,0:T(8,128)(2,1)S(1)}, bf16[2,1,32,384]{3,2,1,0:T(8,128)(2,1)S(1)}, u32[]{:S(2)}, u32[]{:S(2)}) collective-permute-start(bf16[2,1,32,384]{3,2,1,0:T(8,128)(2,1)S(1)} %get-tuple-element.77), channel_id=1, source_target_pairs={{0,1},{2,3},{4,5},{6,7},{8,9},{10,11},{12,13},{14,15},{16,17},{18,... | collective-permute-start | bytes 147464 | tf_op jit(solution)/shard_map/ppermute | solution.py:12
  4.1 20.0 %collective-permute-start.1 = (bf16[2,1,32,384]{3,2,1,0:T(8,128)(2,1)S(1)}, bf16[2,1,32,384]{3,2,1,0:T(8,128)(2,1)S(1)}, u32[]{:S(2)}, u32[]{:S(2)}) collective-permute-start(bf16[2,1,32,384]{3,2,1,0:T(8,128)(2,1)S(1)} %get-tuple-element.78), channel_id=1, source_target_pairs={{1,0},{3,2},{5,4},{7,6},{9,8},{11,10},{13,12},{15,14},{17,16},{19,... | collective-permute-start | bytes 147464 | tf_op jit(solution)/shard_map/ppermute | solution.py:15
  10.7 14.9 %copy-start.7 = (bf16[1,2,4,32,384]{4,3,2,1,0:T(8,128)(2,1)S(1)}, bf16[1,2,4,32,384]{4,3,2,1,0:T(8,128)(2,1)}, u32[]{:S(2)}) copy-start(bf16[1,2,4,32,384]{4,3,2,1,0:T(8,128)(2,1)} %param.8) | copy-start | bytes 589828
  24.2 12.9 %copy-start.4 = (bf16[1,1,3,384,384]{4,3,2,1,0:T(8,128)(2,1)S(1)}, bf16[1,1,3,384,384]{4,3,2,1,0:T(8,128)(2,1)}, u32[]{:S(2)}) copy-start(bf16[1,1,3,384,384]{4,3,2,1,0:T(8,128)(2,1)} %rev.55) | copy-start | bytes 2654212
  24.2 13.4 %copy-start.3 = (bf16[1,1,3,384,384]{4,3,2,1,0:T(8,128)(2,1)S(1)}, bf16[1,1,3,384,384]{4,3,2,1,0:T(8,128)(2,1)}, u32[]{:S(2)}) copy-start(bf16[1,1,3,384,384]{4,3,2,1,0:T(8,128)(2,1)} %rev.56) | copy-start | bytes 2654212
  24.2 11.8 %collective-permute-start.2 = (bf16[2,6,32,384]{3,2,1,0:T(8,128)(2,1)S(1)}, bf16[2,6,32,384]{3,2,1,0:T(8,128)(2,1)S(1)}, u32[]{:S(2)}, u32[]{:S(2)}) collective-permute-start(bf16[2,6,32,384]{3,2,1,0:T(8,128)(2,1)S(1)} %pad_maximum_fusion.19), channel_id=1, source_target_pairs={{2,0},{4,2},{6,4},{3,1},{5,3},{7,5},{10,8},{12,10},{14,12},{11,9},... | collective-permute-start | bytes 884744 | tf_op jit(solution)/shard_map/ppermute | solution.py:23
  25.8 12.5 %copy-start.2 = (bf16[1,1,3,384,384]{4,3,2,1,0:T(8,128)(2,1)S(1)}, bf16[1,1,3,384,384]{4,3,2,1,0:T(8,128)(2,1)}, u32[]{:S(2)}) copy-start(bf16[1,1,3,384,384]{4,3,2,1,0:T(8,128)(2,1)} %rev.57) | copy-start | bytes 2654212
  36.2 2.6 %copy-start.1 = (bf16[1,1,3,384,384]{4,3,2,1,0:T(8,128)(2,1)S(1)}, bf16[1,1,3,384,384]{4,3,2,1,0:T(8,128)(2,1)}, u32[]{:S(2)}) copy-start(bf16[1,1,3,384,384]{4,3,2,1,0:T(8,128)(2,1)} %rev.58) | copy-start | bytes 2654212
  36.9 2.6 %copy-start = (bf16[1,1,3,384,384]{4,3,2,1,0:T(8,128)(2,1)S(1)}, bf16[1,1,3,384,384]{4,3,2,1,0:T(8,128)(2,1)}, u32[]{:S(2)}) copy-start(bf16[1,1,3,384,384]{4,3,2,1,0:T(8,128)(2,1)} %rev.59) | copy-start | bytes 2654212
  38.8 3.0 %copy-start.9 = (bf16[1,1,3,384,384]{4,3,2,1,0:T(8,128)(2,1)S(1)}, bf16[1,1,3,384,384]{4,3,2,1,0:T(8,128)(2,1)}, u32[]{:S(2)}) copy-start(bf16[1,1,3,384,384]{4,3,2,1,0:T(8,128)(2,1)} %rev.54) | copy-start | bytes 2654212
  38.8 3.0 %copy-start.19 = (bf16[1,2,4,32,384]{4,3,2,1,0:T(8,128)(2,1)S(1)}, bf16[1,2,4,32,384]{4,3,2,1,0:T(8,128)(2,1)}, u32[]{:S(2)}) copy-start(bf16[1,2,4,32,384]{4,3,2,1,0:T(8,128)(2,1)} %param.7) | copy-start | bytes 589828
  40.0 9.9 %slice-start = ((s8[7962624]{0:T(1024)(128)(4,1)}), s8[4194304]{0:T(1024)(128)(4,1)S(1)}, s32[]{:S(2)}) async-start(s8[7962624]{0:T(1024)(128)(4,1)} %bitcast.332), calls=%async_computation.1 | async-start | bytes 8388608
  41.2 8.8 %slice-start.1 = ((s8[7962624]{0:T(1024)(128)(4,1)}), s8[3768320]{0:T(1024)(128)(4,1)S(1)}, s32[]{:S(2)}) async-start(s8[7962624]{0:T(1024)(128)(4,1)} %bitcast.332), calls=%async_computation.2 | async-start | bytes 7536640
  42.4 6.1 %copy-start.5 = (bf16[2,4,32,384]{3,2,1,0:T(8,128)(2,1)}, bf16[2,4,32,384]{3,2,1,0:T(8,128)(2,1)S(1)}, u32[]{:S(2)}) copy-start(bf16[2,4,32,384]{3,2,1,0:T(8,128)(2,1)S(1)} %fusion.9) | copy-start | bytes 589828
  42.4 3.5 %collective-permute-start.3 = (bf16[2,1,32,384]{3,2,1,0:T(8,128)(2,1)S(1)}, bf16[2,1,32,384]{3,2,1,0:T(8,128)(2,1)S(1)}, u32[]{:S(2)}, u32[]{:S(2)}) collective-permute-start(bf16[2,1,32,384]{3,2,1,0:T(8,128)(2,1)S(1)} %get-tuple-element.73), channel_id=1, source_target_pairs={{0,1},{2,3},{4,5},{6,7},{8,9},{10,11},{12,13},{14,15},{16,17},{18,... | collective-permute-start | bytes 147464 | tf_op jit(solution)/shard_map/ppermute | solution.py:12
  44.6 3.1 %collective-permute-start.4 = (bf16[2,1,32,384]{3,2,1,0:T(8,128)(2,1)S(1)}, bf16[2,1,32,384]{3,2,1,0:T(8,128)(2,1)S(1)}, u32[]{:S(2)}, u32[]{:S(2)}) collective-permute-start(bf16[2,1,32,384]{3,2,1,0:T(8,128)(2,1)S(1)} %get-tuple-element.74), channel_id=1, source_target_pairs={{1,0},{3,2},{5,4},{7,6},{9,8},{11,10},{13,12},{15,14},{17,16},{19,... | collective-permute-start | bytes 147464 | tf_op jit(solution)/shard_map/ppermute | solution.py:15
  45.9 2.6 %copy-start.16 = (bf16[2,1,32,384]{3,2,1,0:T(8,128)(2,1)}, bf16[2,1,32,384]{3,2,1,0:T(8,128)(2,1)S(1)}, u32[]{:S(2)}) copy-start(bf16[2,1,32,384]{3,2,1,0:T(8,128)(2,1)S(1)} %collective-permute-done.3) | copy-start | bytes 147460
  47.7 0.8 copy-start.17
  48.5 18.6 %collective-permute-start.5 = (bf16[2,6,32,384]{3,2,1,0:T(8,128)(2,1)}, bf16[2,6,32,384]{3,2,1,0:T(8,128)(2,1)}, u32[]{:S(2)}, u32[]{:S(2)}) collective-permute-start(bf16[2,6,32,384]{3,2,1,0:T(8,128)(2,1)} %pad_maximum_fusion.20), channel_id=1, source_target_pairs={{2,0},{4,2},{6,4},{3,1},{5,3},{7,5},{10,8},{12,10},{14,12},{11,9},... | collective-permute-start | bytes 884744 | tf_op jit(solution)/shard_map/ppermute | solution.py:23
  64.7 6.0 %copy-start.6 = (bf16[2,4,32,384]{3,2,1,0:T(8,128)(2,1)S(1)}, bf16[2,4,32,384]{3,2,1,0:T(8,128)(2,1)}, u32[]{:S(2)}) copy-start(bf16[2,4,32,384]{3,2,1,0:T(8,128)(2,1)} %copy-done.5) | copy-start | bytes 589828
  65.9 4.8 %copy-start.15 = (bf16[1,1,3,384,384]{4,3,2,1,0:T(8,128)(2,1)S(1)}, bf16[1,1,3,384,384]{4,3,2,1,0:T(8,128)(2,1)}, u32[]{:S(2)}) copy-start(bf16[1,1,3,384,384]{4,3,2,1,0:T(8,128)(2,1)} %rev.64) | copy-start | bytes 2654212
  65.9 5.4 %copy-start.14 = (bf16[1,1,3,384,384]{4,3,2,1,0:T(8,128)(2,1)S(1)}, bf16[1,1,3,384,384]{4,3,2,1,0:T(8,128)(2,1)}, u32[]{:S(2)}) copy-start(bf16[1,1,3,384,384]{4,3,2,1,0:T(8,128)(2,1)} %rev.65) | copy-start | bytes 2654212
  65.9 5.8 %copy-start.13 = (bf16[1,1,3,384,384]{4,3,2,1,0:T(8,128)(2,1)S(1)}, bf16[1,1,3,384,384]{4,3,2,1,0:T(8,128)(2,1)}, u32[]{:S(2)}) copy-start(bf16[1,1,3,384,384]{4,3,2,1,0:T(8,128)(2,1)} %rev.66) | copy-start | bytes 2654212
  68.2 4.0 %copy-start.12 = (bf16[1,1,3,384,384]{4,3,2,1,0:T(8,128)(2,1)S(1)}, bf16[1,1,3,384,384]{4,3,2,1,0:T(8,128)(2,1)}, u32[]{:S(2)}) copy-start(bf16[1,1,3,384,384]{4,3,2,1,0:T(8,128)(2,1)} %rev.67) | copy-start | bytes 2654212
  68.9 3.9 %copy-start.11 = (bf16[1,1,3,384,384]{4,3,2,1,0:T(8,128)(2,1)S(1)}, bf16[1,1,3,384,384]{4,3,2,1,0:T(8,128)(2,1)}, u32[]{:S(2)}) copy-start(bf16[1,1,3,384,384]{4,3,2,1,0:T(8,128)(2,1)} %rev.68) | copy-start | bytes 2654212
  70.7 3.7 %copy-start.10 = (bf16[1,1,3,384,384]{4,3,2,1,0:T(8,128)(2,1)S(1)}, bf16[1,1,3,384,384]{4,3,2,1,0:T(8,128)(2,1)}, u32[]{:S(2)}) copy-start(bf16[1,1,3,384,384]{4,3,2,1,0:T(8,128)(2,1)} %rev.69) | copy-start | bytes 2654212
  72.2 3.7 %copy-start.8 = (bf16[1,2,4,32,384]{4,3,2,1,0:T(8,128)(2,1)S(1)}, bf16[1,2,4,32,384]{4,3,2,1,0:T(8,128)(2,1)}, u32[]{:S(2)}) copy-start(bf16[1,2,4,32,384]{4,3,2,1,0:T(8,128)(2,1)} %param.8) | copy-start | bytes 589828
  72.3 3.7 %copy-start.18 = (bf16[1,2,4,32,384]{4,3,2,1,0:T(8,128)(2,1)S(1)}, bf16[1,2,4,32,384]{4,3,2,1,0:T(8,128)(2,1)}, u32[]{:S(2)}) copy-start(bf16[1,2,4,32,384]{4,3,2,1,0:T(8,128)(2,1)} %param.6) | copy-start | bytes 589828
where the time goes:
time: 97.7 us; the launch traced here: 96.8 us
  local copies, waits for them, and re-layouts  38.4 us (39%)
  blocking collectives  19.3 us (20%)
  waiting for transfers between devices  12.1 us (12%)
  matrix products  10.2 us (10%)
  starting transfers between devices  10 us (10%)
  other arithmetic  5.43 us (6%)
  between operations  1.33 us (1%)
    rev x18, local copies, waits for them, and re-layouts, transposed_conv(): kernel_slice = kernel[2 - time_tap, 2 - row_tap, ::-1]  26.5 us
    all_to_all x1, blocking collectives, on_device(): lax.all_to_all(result[:, None], ('tm', 'rows'), split_axis=4, concat_axis...  19.3 us
    ppermute x2, waiting for transfers between devices, shifted(): return lax.ppermute(value, axis, pairs)  10.3 us
    dot_general x18, matrix products, transposed_conv(): jnp.einsum('frwkc,kdc->frwd', stacked, kernel_slice, preferred_element_ty...  10.2 us
    slice x2, local copies, waits for them, and re-layouts, transposed_conv(): kernel_slice = kernel[2 - time_tap, 2 - row_tap, ::-1]  8.04 us
    ppermute x2, starting transfers between devices, with_halo(): lax.ppermute(lax.slice_in_dim(block, block.shape[dim] - width, None, axis...  4.57 us
    ppermute x2, starting transfers between devices, shifted(): return lax.ppermute(value, axis, pairs)  2.89 us
    another operation x6, local copies, waits for them, and re-layouts, transposed_conv(): jnp.stack([slab_rows[:, :, col_tap:col_tap + col_count] for col_tap in ra...  2.65 us
  transfers between devices with their start and end apart: 6, of which 2 were waited for; matrix products, arithmetic and copies ran while one was open for 37% of the time, Pallas kernels for 0%

commit v1 on v0

--- a/solution.py
+++ b/solution.py
@@ -2,6 +2,17 @@
 import jax.numpy as jnp
 from jax import lax
 from jax.sharding import PartitionSpec as P
+
+
+def cut_along(x, dim, count):
+    before, after = (x.shape[:dim], x.shape[dim + 1 :])
+    return jnp.moveaxis(x.reshape(*before, count, -1, *after), dim, 0)
+
+
+def laid_out(blocks, dim):
+    lengths = list(blocks.shape[1:])
+    lengths[dim] *= blocks.shape[0]
+    return jnp.moveaxis(blocks, 0, dim).reshape(lengths)
 
 
 def with_halo(block, sides, width):
@@ -72,9 +83,18 @@
     result = result[None]
     time_devs = lax.axis_size("tm")
     row_devs = lax.axis_size("rows")
-    arrived = lax.all_to_all(
-        result[:, None], ("tm", "rows"), split_axis=4, concat_axis=1, tiled=True
-    )
+    value_2 = result[:, None]
+    count_2, here = (lax.axis_size(("tm", "rows")), lax.axis_index(("tm", "rows")))
+    tiles = cut_along(value_2, 4, count_2)
+    out = tiles
+    for step in range(1, count_2):
+        target_2, source_2 = ((here + step) % count_2, (here - step) % count_2)
+        sent = lax.dynamic_index_in_dim(tiles, target_2, 0)
+        partner_block = lax.ppermute(
+            sent, ("tm", "rows"), [(i_2, (i_2 + step) % count_2) for i_2 in range(count_2)]
+        )
+        out = lax.dynamic_update_slice_in_dim(out, partner_block, source_2, axis=0)
+    arrived = laid_out(out, 1)
     col_dev = arrived.shape[4]
     arranged = arrived.reshape(1, time_devs, row_devs, frame_dev, row_dev, col_dev, channels)
     arranged = arranged.transpose(0, 1, 3, 2, 4, 5, 6)

time: 97.7 us -> 92.5 us (0.947)
  blocking collectives: 19.3 us -> 0 us
  starting transfers between devices: 10 us -> 21.1 us
  waiting for transfers between devices: 12.1 us -> 15.1 us
    all_to_all x1 -> x0, blocking collectives: 19.3 us -> none  [on_device(): lax.all_to_all(result[:, None], ('tm', 'rows'), split_axis=4, concat_axis...]
    ppermute x0 -> x7, starting transfers between devices: none -> 11.1 us  [on_device(): lax.ppermute(sent, ('tm', 'rows'), [(i_2, (i_2 + step) % count_2) for i_2...]
    ppermute x0 -> x7, waiting for transfers between devices: none -> 3.06 us  [on_device(): lax.ppermute(sent, ('tm', 'rows'), [(i_2, (i_2 + step) % count_2) for i_2...]
  transfers between devices with their start and end apart: 6 -> 13, of which waited for: 2 -> 4; matrix products, arithmetic and copies ran while one was open for 37% -> 39% of each run, Pallas kernels for 0% -> 0%
where the time goes in v1:
time: 92.5 us; the launch traced here: 91.8 us
  local copies, waits for them, and re-layouts  38.5 us (42%)
  starting transfers between devices  21.1 us (23%)
  waiting for transfers between devices  15.1 us (16%)
  matrix products  10.2 us (11%)
  other arithmetic  5.43 us (6%)
  between operations  1.43 us (2%)
    rev x18, local copies, waits for them, and re-layouts, transposed_conv(): kernel_slice = kernel[2 - time_tap, 2 - row_tap, ::-1]  26.5 us
    ppermute x7, starting transfers between devices, on_device(): lax.ppermute(sent, ('tm', 'rows'), [(i_2, (i_2 + step) % count_2) for i_2...  11.1 us
    ppermute x2, waiting for transfers between devices, shifted(): return lax.ppermute(value, axis, pairs)  10.3 us
    dot_general x18, matrix products, transposed_conv(): jnp.einsum('frwkc,kdc->frwd', stacked, kernel_slice, preferred_element_ty...  10.2 us
    slice x2, local copies, waits for them, and re-layouts, transposed_conv(): kernel_slice = kernel[2 - time_tap, 2 - row_tap, ::-1]  8.07 us
    ppermute x2, starting transfers between devices, with_halo(): lax.ppermute(lax.slice_in_dim(block, block.shape[dim] - width, None, axis...  4.57 us
    ppermute x7, waiting for transfers between devices, on_device(): lax.ppermute(sent, ('tm', 'rows'), [(i_2, (i_2 + step) % count_2) for i_2...  3.06 us
    ppermute x2, starting transfers between devices, shifted(): return lax.ppermute(value, axis, pairs)  2.89 us
  transfers between devices with their start and end apart: 13, of which 4 were waited for; matrix products, arithmetic and copies ran while one was open for 39% of the time, Pallas kernels for 0%

profile of v1, /device:TPU:0, one launch (start us, length us, event | category | flops | bytes accessed | tf_op | source)
XLA Modules:
  0.0 91.8 jit_solution(4524141723642575432)
XLA Ops:
  0.7 1.0 %bitcast_select_fusion.1 = bf16[2,4,32,384]{3,2,1,0:T(8,128)(2,1)S(1)} fusion(bf16[1,2,4,32,384]{4,3,2,1,0:T(8,128)(2,1)} %param.8, pred[2]{0:T(512)(128)(4,1)S(1)} %add_compare_fusion), kind=kLoop, calls=%fused_computation.206 | loop fusion | flops 98304 | bytes 393218 | tf_op jit(solution)/shard_map/jit(_where)/select_n | solution.py:70
  1.7 2.4 %collective-permute-start = (bf16[2,1,32,384]{3,2,1,0:T(8,128)(2,1)S(1)}, bf16[2,1,32,384]{3,2,1,0:T(8,128)(2,1)S(1)}, u32[]{:S(2)}, u32[]{:S(2)}) collective-permute-start(bf16[2,1,32,384]{3,2,1,0:T(8,128)(2,1)S(1)} %get-tuple-element.84), channel_id=1, source_target_pairs={{0,1},{2,3},{4,5},{6,7},{8,9},{10,11},{12,13},{14,15},{16,17},{18,... | collective-permute-start | bytes 147464 | tf_op jit(solution)/shard_map/ppermute | solution.py:23
  4.1 1.3 %collective-permute-start.1 = (bf16[2,1,32,384]{3,2,1,0:T(8,128)(2,1)S(1)}, bf16[2,1,32,384]{3,2,1,0:T(8,128)(2,1)S(1)}, u32[]{:S(2)}, u32[]{:S(2)}) collective-permute-start(bf16[2,1,32,384]{3,2,1,0:T(8,128)(2,1)S(1)} %get-tuple-element.85), channel_id=1, source_target_pairs={{1,0},{3,2},{5,4},{7,6},{9,8},{11,10},{13,12},{15,14},{17,16},{19,... | collective-permute-start | bytes 147464 | tf_op jit(solution)/shard_map/ppermute | solution.py:26
  5.4 5.3 %fusion.121 = (bf16[1,1,3,384,384]{4,3,2,1,0:T(8,128)(2,1)S(1)}, bf16[1,1,3,384,384]{4,3,2,1,0:T(8,128)(2,1)}, bf16[1,1,3,384,384]{4,3,2,1,0:T(8,128)(2,1)}, bf1...) fusion(bf16[3,3,3,384,384]{4,3,2,1,0:T(8,128)(2,1)} %param.10), kind=kLoop, calls=%fused_computation.224 | loop fusion | bytes 15925248 | tf_op jit(solution)/shard_map/slice | solution.py:55
  10.7 2.2 %rev.57 = bf16[1,1,3,384,384]{4,3,2,1,0:T(8,128)(2,1)} reverse(bf16[1,1,3,384,384]{4,3,2,1,0:T(8,128)(2,1)} %get-tuple-element.18), dimensions={2} | reverse | bytes 1769472 | tf_op jit(solution)/shard_map/rev | solution.py:55
  12.9 2.2 %rev.58 = bf16[1,1,3,384,384]{4,3,2,1,0:T(8,128)(2,1)} reverse(bf16[1,1,3,384,384]{4,3,2,1,0:T(8,128)(2,1)} %get-tuple-element.17), dimensions={2} | reverse | bytes 1769472 | tf_op jit(solution)/shard_map/rev | solution.py:55
  15.1 2.2 %rev.59 = bf16[1,1,3,384,384]{4,3,2,1,0:T(8,128)(2,1)} reverse(bf16[1,1,3,384,384]{4,3,2,1,0:T(8,128)(2,1)} %get-tuple-element.16), dimensions={2} | reverse | bytes 1769472 | tf_op jit(solution)/shard_map/rev | solution.py:55
  17.3 2.2 %rev.60 = bf16[1,1,3,384,384]{4,3,2,1,0:T(8,128)(2,1)} reverse(bf16[1,1,3,384,384]{4,3,2,1,0:T(8,128)(2,1)} %get-tuple-element.15), dimensions={2} | reverse | bytes 1769472 | tf_op jit(solution)/shard_map/rev | solution.py:55
  19.5 1.0 %rev.61 = bf16[1,1,3,384,384]{4,3,2,1,0:T(8,128)(2,1)} reverse(bf16[1,1,3,384,384]{4,3,2,1,0:T(8,128)(2,1)S(1)} %get-tuple-element.22), dimensions={2} | reverse | bytes 1769472 | tf_op jit(solution)/shard_map/rev | solution.py:55
  20.7 1.3 %rev.56 = bf16[1,1,3,384,384]{4,3,2,1,0:T(8,128)(2,1)S(1)} reverse(bf16[1,1,3,384,384]{4,3,2,1,0:T(8,128)(2,1)} %get-tuple-element.19), dimensions={2} | reverse | bytes 1769472 | tf_op jit(solution)/shard_map/rev | solution.py:55
  22.0 2.2 %rev.54 = bf16[1,1,3,384,384]{4,3,2,1,0:T(8,128)(2,1)} reverse(bf16[1,1,3,384,384]{4,3,2,1,0:T(8,128)(2,1)} %get-tuple-element.20), dimensions={2} | reverse | bytes 1769472 | tf_op jit(solution)/shard_map/rev | solution.py:55
  24.2 1.4 %collective-permute-start.2 = (bf16[2,6,32,384]{3,2,1,0:T(8,128)(2,1)S(1)}, bf16[2,6,32,384]{3,2,1,0:T(8,128)(2,1)S(1)}, u32[]{:S(2)}, u32[]{:S(2)}) collective-permute-start(bf16[2,6,32,384]{3,2,1,0:T(8,128)(2,1)S(1)} %pad_maximum_fusion.19), channel_id=1, source_target_pairs={{2,0},{4,2},{6,4},{3,1},{5,3},{7,5},{10,8},{12,10},{14,12},{11,9},... | collective-permute-start | bytes 884744 | tf_op jit(solution)/shard_map/ppermute | solution.py:34
  25.8 10.3 %collective-permute-done.2 = bf16[2,6,32,384]{3,2,1,0:T(8,128)(2,1)S(1)} collective-permute-done((bf16[2,6,32,384]{3,2,1,0:T(8,128)(2,1)S(1)}, bf16[2,6,32,384]{3,2,1,0:T(8,128)(2,1)S(1)}, u32[]{:S(2)}, u32[]{:S(2)}) %collective-permute-start.2) | collective-permute-done | bytes 294944 | tf_op jit(solution)/shard_map/ppermute | solution.py:34
  36.2 0.7 fusion.81
  36.9 0.2 pad_maximum_fusion.3
  37.1 0.5 fusion.38
  37.6 0.5 fusion.36
  38.2 0.2 pad_maximum_fusion.5
  38.4 0.5 fusion.34
  38.9 0.5 fusion.32
  39.4 0.2 pad_maximum_fusion.7
  39.5 0.5 fusion.30
  40.1 0.5 fusion.28
  40.5 0.2 pad_maximum_fusion.1
  40.7 0.5 fusion.42
  41.2 0.5 fusion.40
  41.7 0.7 fusion.9
  42.4 2.2 %collective-permute-start.3 = (bf16[2,1,32,384]{3,2,1,0:T(8,128)(2,1)S(1)}, bf16[2,1,32,384]{3,2,1,0:T(8,128)(2,1)S(1)}, u32[]{:S(2)}, u32[]{:S(2)}) collective-permute-start(bf16[2,1,32,384]{3,2,1,0:T(8,128)(2,1)S(1)} %get-tuple-element.80), channel_id=1, source_target_pairs={{0,1},{2,3},{4,5},{6,7},{8,9},{10,11},{12,13},{14,15},{16,17},{18,... | collective-permute-start | bytes 147464 | tf_op jit(solution)/shard_map/ppermute | solution.py:23
  44.6 1.3 %collective-permute-start.4 = (bf16[2,1,32,384]{3,2,1,0:T(8,128)(2,1)S(1)}, bf16[2,1,32,384]{3,2,1,0:T(8,128)(2,1)S(1)}, u32[]{:S(2)}, u32[]{:S(2)}) collective-permute-start(bf16[2,1,32,384]{3,2,1,0:T(8,128)(2,1)S(1)} %get-tuple-element.81), channel_id=1, source_target_pairs={{1,0},{3,2},{5,4},{7,6},{9,8},{11,10},{13,12},{15,14},{17,16},{19,... | collective-permute-start | bytes 147464 | tf_op jit(solution)/shard_map/ppermute | solution.py:26
  45.9 1.8 %collective-permute-done.4 = bf16[2,1,32,384]{3,2,1,0:T(8,128)(2,1)S(1)} collective-permute-done((bf16[2,1,32,384]{3,2,1,0:T(8,128)(2,1)S(1)}, bf16[2,1,32,384]{3,2,1,0:T(8,128)(2,1)S(1)}, u32[]{:S(2)}, u32[]{:S(2)}) %collective-permute-start.4) | collective-permute-done | bytes 49184 | tf_op jit(solution)/shard_map/ppermute | solution.py:26
  47.7 0.8 pad_maximum_fusion.20
  48.5 1.5 %collective-permute-start.5 = (bf16[2,6,32,384]{3,2,1,0:T(8,128)(2,1)}, bf16[2,6,32,384]{3,2,1,0:T(8,128)(2,1)}, u32[]{:S(2)}, u32[]{:S(2)}) collective-permute-start(bf16[2,6,32,384]{3,2,1,0:T(8,128)(2,1)} %pad_maximum_fusion.20), channel_id=1, source_target_pairs={{2,0},{4,2},{6,4},{3,1},{5,3},{7,5},{10,8},{12,10},{14,12},{11,9},... | collective-permute-start | bytes 884744 | tf_op jit(solution)/shard_map/ppermute | solution.py:34
  50.0 2.8 %fusion.120 = (bf16[1,1,3,384,384]{4,3,2,1,0:T(8,128)(2,1)}, bf16[1,1,3,384,384]{4,3,2,1,0:T(8,128)(2,1)S(1)}, bf16[1,1,3,384,384]{4,3,2,1,0:T(8,128)(2,1)S(1)},...) fusion(bf16[3,3,3,384,384]{4,3,2,1,0:T(8,128)(2,1)S(1)} %bitcas, ...), kind=kLoop, calls=%fused_computation.223 | loop fusion | bytes 15925248 | tf_op jit(solution)/shard_map/slice | solution.py:55
  52.8 2.2 %rev.63 = bf16[1,1,3,384,384]{4,3,2,1,0:T(8,128)(2,1)} reverse(bf16[1,1,3,384,384]{4,3,2,1,0:T(8,128)(2,1)} %get-tuple-element.5), dimensions={2} | reverse | bytes 1769472 | tf_op jit(solution)/shard_map/rev | solution.py:55
  54.9 2.2 %rev.64 = bf16[1,1,3,384,384]{4,3,2,1,0:T(8,128)(2,1)} reverse(bf16[1,1,3,384,384]{4,3,2,1,0:T(8,128)(2,1)} %get-tuple-element.11), dimensions={2} | reverse | bytes 1769472 | tf_op jit(solution)/shard_map/rev | solution.py:55
  57.1 2.2 %rev.65 = bf16[1,1,3,384,384]{4,3,2,1,0:T(8,128)(2,1)} reverse(bf16[1,1,3,384,384]{4,3,2,1,0:T(8,128)(2,1)} %get-tuple-element.10), dimensions={2} | reverse | bytes 1769472 | tf_op jit(solution)/shard_map/rev | solution.py:55
  59.3 2.2 %rev.66 = bf16[1,1,3,384,384]{4,3,2,1,0:T(8,128)(2,1)} reverse(bf16[1,1,3,384,384]{4,3,2,1,0:T(8,128)(2,1)} %get-tuple-element.9), dimensions={2} | reverse | bytes 1769472 | tf_op jit(solution)/shard_map/rev | solution.py:55
  61.5 2.2 %rev.67 = bf16[1,1,3,384,384]{4,3,2,1,0:T(8,128)(2,1)} reverse(bf16[1,1,3,384,384]{4,3,2,1,0:T(8,128)(2,1)} %get-tuple-element.8), dimensions={2} | reverse | bytes 1769472 | tf_op jit(solution)/shard_map/rev | solution.py:55
  63.7 1.0 %rev.68 = bf16[1,1,3,384,384]{4,3,2,1,0:T(8,128)(2,1)} reverse(bf16[1,1,3,384,384]{4,3,2,1,0:T(8,128)(2,1)S(1)} %get-tuple-element.7), dimensions={2} | reverse | bytes 1769472 | tf_op jit(solution)/shard_map/rev | solution.py:55
  64.7 1.0 %rev.69 = bf16[1,1,3,384,384]{4,3,2,1,0:T(8,128)(2,1)} reverse(bf16[1,1,3,384,384]{4,3,2,1,0:T(8,128)(2,1)S(1)} %get-tuple-element.6), dimensions={2} | reverse | bytes 1769472 | tf_op jit(solution)/shard_map/rev | solution.py:55
  66.0 1.2 %fusion.116 = (bf16[2,4,32,1,384]{4,2,1,0,3:T(8,128)(2,1)S(1)}, bf16[2,4,32,1,384]{4,2,1,0,3:T(8,128)(2,1)S(1)}) fusion(bf16[2,4,32,384]{3,2,1,0:T(8,128)(2,1)} %copy-done.5, bf16[2,1,32,384]{3,2,1,0:T(8,128)(2,1)} %copy-done.16, bf16[2,1,32,384]{3,2,1,0:T(8,128)(2,1)} %copy-done.17), kind=kLoop, calls=%fused_computation.194 | loop fusion | flops 196608 | bytes 688128 | tf_op jit(solution)/shard_map/stack | solution.py:52
  67.2 1.1 %pad_maximum_fusion.9 = bf16[4,6,32,384]{3,2,1,0:T(8,128)(2,1)S(1)} fusion(bf16[2,6,32,384]{3,2,1,0:T(8,128)(2,1)} %collective-permute-done.5, bf16[2,1,32,384]{3,2,1,0:T(8,128)(2,1)} %copy-done.17, bf16[2,4,32,384]{3,2,1,0:T(8,128)(2,1)} %copy-done.5, bf16[2,1,32,384]{3,2,1,0:T(8,128)(2,1)} %copy-done.16), kind=kLoop, calls=%fused_computation.60 | loop fusion | flops 884736 | bytes 1179648 | tf_op jit(solution)/shard_map/concatenate | solution.py:43
  68.3 0.7 fusion.97
  69.1 1.7 %fusion.26 = f32[2,4,32,384,1]{3,2,0,1,4:T(8,128)S(1)} fusion(bf16[1,1,3,384,384]{4,3,2,1,0:T(8,128)(2,1)} %rev.63, bf16[2,4,32,1,384]{4,2,1,0,3:T(8,128)(2,1)S(1)} %get-tuple-element.24, bf16[2,4,32,1,384]{4,2,1,0,3:T(8,128)(2,1)S(1)} %get-tuple-element.78, bf16[2,4,32,1,384]{4,2,1,0,3:T(8,128)(2,1)S(1)} %get-tuple-element.23), kind=kOutput, calls=%fused_computation.27 | convolution fusion | flops 227082240 | bytes 1867776 | tf_op jit(solution)/shard_map/frwkc,kdc->frwd/dot_general | solution.py:56
  70.8 0.5 fusion.24
  71.3 0.5 fusion.22
  71.8 0.5 fusion.20
  72.4 0.5 fusion.18
  72.9 0.5 fusion.16
  73.4 1.2 %slice_bitcast_fusion.2 = (bf16[2,4,32,1,384]{4,2,1,0,3:T(8,128)(2,1)S(1)}, bf16[2,4,32,1,384]{4,2,1,0,3:T(8,128)(2,1)S(1)}, bf16[2,4,32,1,384]{4,2,1,0,3:T(8,128)(2,1)S(1)}) fusion(bf16[2,6,32,384]{3,2,1,0:T(8,128)(2,1)} %collective-permute-done.5), kind=kLoop, calls=%fused_computation.187 | loop fusion | bytes 1179648 | tf_op jit(solution)/shard_map/stack | solution.py:52
  74.6 0.5 fusion.14
  75.1 0.5 fusion.12
  75.6 0.5 fusion.10
  76.1 0.4 fusion.78
  76.7 0.2 collective-permute-start.6
  76.9 2.8 %collective-permute-start.7 = (f32[1,1,1,2,4,4,384]{6,5,0,4,3,2,1:T(4,128)S(1)}, f32[1,1,1,2,4,4,384]{6,5,0,4,3,2,1:T(4,128)S(1)}, u32[]{:S(2)}, u32[]{:S(2)}) collective-permute-start(f32[1,1,1,2,4,4,384]{6,5,0,4,3,2,1:T(4,128)S(1)} %get-tuple-element.70), channel_id=1, source_target_pairs={{0,2},{1,3},{2,4},{3,5},{4,6},{5,7},{6,0},{7,1},{8,10},{9,11},{10,... | collective-permute-start | bytes 147464 | tf_op jit(solution)/shard_map/ppermute | solution.py:93
  79.7 3.3 %collective-permute-start.8 = (f32[1,1,1,2,4,4,384]{6,5,0,4,3,2,1:T(4,128)S(1)}, f32[1,1,1,2,4,4,384]{6,5,0,4,3,2,1:T(4,128)S(1)}, u32[]{:S(2)}, u32[]{:S(2)}) collective-permute-start(f32[1,1,1,2,4,4,384]{6,5,0,4,3,2,1:T(4,128)S(1)} %get-tuple-element.69), channel_id=1, source_target_pairs={{0,3},{1,4},{2,5},{3,6},{4,7},{5,0},{6,1},{7,2},{8,11},{9,12},{10,... | collective-permute-start | bytes 147464 | tf_op jit(solution)/shard_map/ppermute | solution.py:93
  83.0 0.3 collective-permute-start.9
  83.3 2.3 %collective-permute-start.10 = (f32[1,1,1,2,4,4,384]{6,5,0,4,3,2,1:T(4,128)S(1)}, f32[1,1,1,2,4,4,384]{6,5,0,4,3,2,1:T(4,128)S(1)}, u32[]{:S(2)}, u32[]{:S(2)}) collective-permute-start(f32[1,1,1,2,4,4,384]{6,5,0,4,3,2,1:T(4,128)S(1)} %get-tuple-element.67), channel_id=1, source_target_pairs={{0,5},{1,6},{2,7},{3,0},{4,1},{5,2},{6,3},{7,4},{8,13},{9,14},{10,... | collective-permute-start | bytes 147464 | tf_op jit(solution)/shard_map/ppermute | solution.py:93
  85.6 0.8 collective-permute-start.11
  86.5 1.3 %collective-permute-start.12 = (f32[1,1,1,2,4,4,384]{6,5,0,4,3,2,1:T(4,128)S(1)}, f32[1,1,1,2,4,4,384]{6,5,0,4,3,2,1:T(4,128)S(1)}, u32[]{:S(2)}, u32[]{:S(2)}) collective-permute-start(f32[1,1,1,2,4,4,384]{6,5,0,4,3,2,1:T(4,128)S(1)} %get-tuple-element.65), channel_id=1, source_target_pairs={{0,7},{1,0},{2,1},{3,2},{4,3},{5,4},{6,5},{7,6},{8,15},{9,8},{10,9... | collective-permute-start | bytes 147464 | tf_op jit(solution)/shard_map/ppermute | solution.py:93
  87.8 1.7 %collective-permute-done.9 = f32[1,1,1,2,4,4,384]{6,5,0,4,3,2,1:T(4,128)S(1)} collective-permute-done((f32[1,1,1,2,4,4,384]{6,5,0,4,3,2,1:T(4,128)S(1)}, f32[1,1,1,2,4,4,384]{6,5,0,4,3,2,1:T(4,128)S(1)}, u32[]{:S(2)}, u32[]{:S(2)}) %collective-permute-start.9) | collective-permute-done | bytes 49184 | tf_op jit(solution)/shard_map/ppermute | solution.py:93
  89.6 1.3 %collective-permute-done.11 = f32[1,1,1,2,4,4,384]{6,5,0,4,3,2,1:T(4,128)S(1)} collective-permute-done((f32[1,1,1,2,4,4,384]{6,5,0,4,3,2,1:T(4,128)S(1)}, f32[1,1,1,2,4,4,384]{6,5,0,4,3,2,1:T(4,128)S(1)}, u32[]{:S(2)}, u32[]{:S(2)}) %collective-permute-start.11) | collective-permute-done | bytes 49184 | tf_op jit(solution)/shard_map/ppermute | solution.py:93
  91.0 0.8 copy.26
  (77 shorter events, 1.2 us)
Async XLA Ops:
  1.7 22.4 %collective-permute-start = (bf16[2,1,32,384]{3,2,1,0:T(8,128)(2,1)S(1)}, bf16[2,1,32,384]{3,2,1,0:T(8,128)(2,1)S(1)}, u32[]{:S(2)}, u32[]{:S(2)}) collective-permute-start(bf16[2,1,32,384]{3,2,1,0:T(8,128)(2,1)S(1)} %get-tuple-element.84), channel_id=1, source_target_pairs={{0,1},{2,3},{4,5},{6,7},{8,9},{10,11},{12,13},{14,15},{16,17},{18,... | collective-permute-start | bytes 147464 | tf_op jit(solution)/shard_map/ppermute | solution.py:23
  4.1 20.0 %collective-permute-start.1 = (bf16[2,1,32,384]{3,2,1,0:T(8,128)(2,1)S(1)}, bf16[2,1,32,384]{3,2,1,0:T(8,128)(2,1)S(1)}, u32[]{:S(2)}, u32[]{:S(2)}) collective-permute-start(bf16[2,1,32,384]{3,2,1,0:T(8,128)(2,1)S(1)} %get-tuple-element.85), channel_id=1, source_target_pairs={{1,0},{3,2},{5,4},{7,6},{9,8},{11,10},{13,12},{15,14},{17,16},{19,... | collective-permute-start | bytes 147464 | tf_op jit(solution)/shard_map/ppermute | solution.py:26
  10.7 14.9 %copy-start.7 = (bf16[1,2,4,32,384]{4,3,2,1,0:T(8,128)(2,1)S(1)}, bf16[1,2,4,32,384]{4,3,2,1,0:T(8,128)(2,1)}, u32[]{:S(2)}) copy-start(bf16[1,2,4,32,384]{4,3,2,1,0:T(8,128)(2,1)} %param.8) | copy-start | bytes 589828
  24.1 12.9 %copy-start.4 = (bf16[1,1,3,384,384]{4,3,2,1,0:T(8,128)(2,1)S(1)}, bf16[1,1,3,384,384]{4,3,2,1,0:T(8,128)(2,1)}, u32[]{:S(2)}) copy-start(bf16[1,1,3,384,384]{4,3,2,1,0:T(8,128)(2,1)} %rev.57) | copy-start | bytes 2654212
  24.2 13.4 %copy-start.3 = (bf16[1,1,3,384,384]{4,3,2,1,0:T(8,128)(2,1)S(1)}, bf16[1,1,3,384,384]{4,3,2,1,0:T(8,128)(2,1)}, u32[]{:S(2)}) copy-start(bf16[1,1,3,384,384]{4,3,2,1,0:T(8,128)(2,1)} %rev.58) | copy-start | bytes 2654212
  24.2 11.8 %collective-permute-start.2 = (bf16[2,6,32,384]{3,2,1,0:T(8,128)(2,1)S(1)}, bf16[2,6,32,384]{3,2,1,0:T(8,128)(2,1)S(1)}, u32[]{:S(2)}, u32[]{:S(2)}) collective-permute-start(bf16[2,6,32,384]{3,2,1,0:T(8,128)(2,1)S(1)} %pad_maximum_fusion.19), channel_id=1, source_target_pairs={{2,0},{4,2},{6,4},{3,1},{5,3},{7,5},{10,8},{12,10},{14,12},{11,9},... | collective-permute-start | bytes 884744 | tf_op jit(solution)/shard_map/ppermute | solution.py:34
  36.2 2.2 %copy-start.2 = (bf16[1,1,3,384,384]{4,3,2,1,0:T(8,128)(2,1)S(1)}, bf16[1,1,3,384,384]{4,3,2,1,0:T(8,128)(2,1)}, u32[]{:S(2)}) copy-start(bf16[1,1,3,384,384]{4,3,2,1,0:T(8,128)(2,1)} %rev.59) | copy-start | bytes 2654212
  36.2 2.7 %copy-start.1 = (bf16[1,1,3,384,384]{4,3,2,1,0:T(8,128)(2,1)S(1)}, bf16[1,1,3,384,384]{4,3,2,1,0:T(8,128)(2,1)}, u32[]{:S(2)}) copy-start(bf16[1,1,3,384,384]{4,3,2,1,0:T(8,128)(2,1)} %rev.60) | copy-start | bytes 2654212
  36.9 2.6 %copy-start = (bf16[1,1,3,384,384]{4,3,2,1,0:T(8,128)(2,1)S(1)}, bf16[1,1,3,384,384]{4,3,2,1,0:T(8,128)(2,1)}, u32[]{:S(2)}) copy-start(bf16[1,1,3,384,384]{4,3,2,1,0:T(8,128)(2,1)} %rev.61) | copy-start | bytes 2654212
  38.3 3.4 %copy-start.9 = (bf16[1,1,3,384,384]{4,3,2,1,0:T(8,128)(2,1)S(1)}, bf16[1,1,3,384,384]{4,3,2,1,0:T(8,128)(2,1)}, u32[]{:S(2)}) copy-start(bf16[1,1,3,384,384]{4,3,2,1,0:T(8,128)(2,1)} %rev.54) | copy-start | bytes 2654212
  38.4 3.4 %copy-start.19 = (bf16[1,2,4,32,384]{4,3,2,1,0:T(8,128)(2,1)S(1)}, bf16[1,2,4,32,384]{4,3,2,1,0:T(8,128)(2,1)}, u32[]{:S(2)}) copy-start(bf16[1,2,4,32,384]{4,3,2,1,0:T(8,128)(2,1)} %param.7) | copy-start | bytes 589828
  40.0 9.9 %slice-start = ((s8[7962624]{0:T(1024)(128)(4,1)}), s8[4194304]{0:T(1024)(128)(4,1)S(1)}, s32[]{:S(2)}) async-start(s8[7962624]{0:T(1024)(128)(4,1)} %bitcast.343), calls=%async_computation | async-start | bytes 8388608
  41.2 8.8 %slice-start.1 = ((s8[7962624]{0:T(1024)(128)(4,1)}), s8[3768320]{0:T(1024)(128)(4,1)S(1)}, s32[]{:S(2)}) async-start(s8[7962624]{0:T(1024)(128)(4,1)} %bitcast.343), calls=%async_computation.1 | async-start | bytes 7536640
  42.4 6.1 %copy-start.5 = (bf16[2,4,32,384]{3,2,1,0:T(8,128)(2,1)}, bf16[2,4,32,384]{3,2,1,0:T(8,128)(2,1)S(1)}, u32[]{:S(2)}) copy-start(bf16[2,4,32,384]{3,2,1,0:T(8,128)(2,1)S(1)} %fusion.9) | copy-start | bytes 589828
  42.4 3.5 %collective-permute-start.3 = (bf16[2,1,32,384]{3,2,1,0:T(8,128)(2,1)S(1)}, bf16[2,1,32,384]{3,2,1,0:T(8,128)(2,1)S(1)}, u32[]{:S(2)}, u32[]{:S(2)}) collective-permute-start(bf16[2,1,32,384]{3,2,1,0:T(8,128)(2,1)S(1)} %get-tuple-element.80), channel_id=1, source_target_pairs={{0,1},{2,3},{4,5},{6,7},{8,9},{10,11},{12,13},{14,15},{16,17},{18,... | collective-permute-start | bytes 147464 | tf_op jit(solution)/shard_map/ppermute | solution.py:23
  44.6 3.1 %collective-permute-start.4 = (bf16[2,1,32,384]{3,2,1,0:T(8,128)(2,1)S(1)}, bf16[2,1,32,384]{3,2,1,0:T(8,128)(2,1)S(1)}, u32[]{:S(2)}, u32[]{:S(2)}) collective-permute-start(bf16[2,1,32,384]{3,2,1,0:T(8,128)(2,1)S(1)} %get-tuple-element.81), channel_id=1, source_target_pairs={{1,0},{3,2},{5,4},{7,6},{9,8},{11,10},{13,12},{15,14},{17,16},{19,... | collective-permute-start | bytes 147464 | tf_op jit(solution)/shard_map/ppermute | solution.py:26
  45.9 2.6 %copy-start.16 = (bf16[2,1,32,384]{3,2,1,0:T(8,128)(2,1)}, bf16[2,1,32,384]{3,2,1,0:T(8,128)(2,1)S(1)}, u32[]{:S(2)}) copy-start(bf16[2,1,32,384]{3,2,1,0:T(8,128)(2,1)S(1)} %collective-permute-done.3) | copy-start | bytes 147460
  47.7 0.8 copy-start.17
  48.5 18.7 %collective-permute-start.5 = (bf16[2,6,32,384]{3,2,1,0:T(8,128)(2,1)}, bf16[2,6,32,384]{3,2,1,0:T(8,128)(2,1)}, u32[]{:S(2)}, u32[]{:S(2)}) collective-permute-start(bf16[2,6,32,384]{3,2,1,0:T(8,128)(2,1)} %pad_maximum_fusion.20), channel_id=1, source_target_pairs={{2,0},{4,2},{6,4},{3,1},{5,3},{7,5},{10,8},{12,10},{14,12},{11,9},... | collective-permute-start | bytes 884744 | tf_op jit(solution)/shard_map/ppermute | solution.py:34
  64.7 6.1 %copy-start.6 = (bf16[2,4,32,384]{3,2,1,0:T(8,128)(2,1)S(1)}, bf16[2,4,32,384]{3,2,1,0:T(8,128)(2,1)}, u32[]{:S(2)}) copy-start(bf16[2,4,32,384]{3,2,1,0:T(8,128)(2,1)} %copy-done.5) | copy-start | bytes 589828
  65.9 5.4 %copy-start.14 = (bf16[1,1,3,384,384]{4,3,2,1,0:T(8,128)(2,1)S(1)}, bf16[1,1,3,384,384]{4,3,2,1,0:T(8,128)(2,1)}, u32[]{:S(2)}) copy-start(bf16[1,1,3,384,384]{4,3,2,1,0:T(8,128)(2,1)} %rev.65) | copy-start | bytes 2654212
  66.0 4.8 %copy-start.15 = (bf16[1,1,3,384,384]{4,3,2,1,0:T(8,128)(2,1)S(1)}, bf16[1,1,3,384,384]{4,3,2,1,0:T(8,128)(2,1)}, u32[]{:S(2)}) copy-start(bf16[1,1,3,384,384]{4,3,2,1,0:T(8,128)(2,1)} %rev.64) | copy-start | bytes 2654212
  66.0 5.8 %copy-start.13 = (bf16[1,1,3,384,384]{4,3,2,1,0:T(8,128)(2,1)S(1)}, bf16[1,1,3,384,384]{4,3,2,1,0:T(8,128)(2,1)}, u32[]{:S(2)}) copy-start(bf16[1,1,3,384,384]{4,3,2,1,0:T(8,128)(2,1)} %rev.66) | copy-start | bytes 2654212
  68.3 4.0 %copy-start.12 = (bf16[1,1,3,384,384]{4,3,2,1,0:T(8,128)(2,1)S(1)}, bf16[1,1,3,384,384]{4,3,2,1,0:T(8,128)(2,1)}, u32[]{:S(2)}) copy-start(bf16[1,1,3,384,384]{4,3,2,1,0:T(8,128)(2,1)} %rev.67) | copy-start | bytes 2654212
  69.0 3.9 %copy-start.11 = (bf16[1,1,3,384,384]{4,3,2,1,0:T(8,128)(2,1)S(1)}, bf16[1,1,3,384,384]{4,3,2,1,0:T(8,128)(2,1)}, u32[]{:S(2)}) copy-start(bf16[1,1,3,384,384]{4,3,2,1,0:T(8,128)(2,1)} %rev.68) | copy-start | bytes 2654212
  70.8 3.7 %copy-start.10 = (bf16[1,1,3,384,384]{4,3,2,1,0:T(8,128)(2,1)S(1)}, bf16[1,1,3,384,384]{4,3,2,1,0:T(8,128)(2,1)}, u32[]{:S(2)}) copy-start(bf16[1,1,3,384,384]{4,3,2,1,0:T(8,128)(2,1)} %rev.69) | copy-start | bytes 2654212
  72.3 3.7 %copy-start.8 = (bf16[1,2,4,32,384]{4,3,2,1,0:T(8,128)(2,1)S(1)}, bf16[1,2,4,32,384]{4,3,2,1,0:T(8,128)(2,1)}, u32[]{:S(2)}) copy-start(bf16[1,2,4,32,384]{4,3,2,1,0:T(8,128)(2,1)} %param.8) | copy-start | bytes 589828
  72.4 3.7 %copy-start.18 = (bf16[1,2,4,32,384]{4,3,2,1,0:T(8,128)(2,1)S(1)}, bf16[1,2,4,32,384]{4,3,2,1,0:T(8,128)(2,1)}, u32[]{:S(2)}) copy-start(bf16[1,2,4,32,384]{4,3,2,1,0:T(8,128)(2,1)} %param.6) | copy-start | bytes 589828
  76.7 8.9 %collective-permute-start.6 = (f32[1,1,1,2,4,4,384]{6,5,0,4,3,2,1:T(4,128)S(1)}, f32[1,1,1,2,4,4,384]{6,5,0,4,3,2,1:T(4,128)S(1)}, u32[]{:S(2)}, u32[]{:S(2)}) collective-permute-start(f32[1,1,1,2,4,4,384]{6,5,0,4,3,2,1:T(4,128)S(1)} %get-tuple-element.71), channel_id=1, source_target_pairs={{0,1},{1,2},{2,3},{3,4},{4,5},{5,6},{6,7},{7,0},{8,9},{9,10},{10,1... | collective-permute-start | bytes 147464 | tf_op jit(solution)/shard_map/ppermute | solution.py:93
  76.9 9.6 %collective-permute-start.7 = (f32[1,1,1,2,4,4,384]{6,5,0,4,3,2,1:T(4,128)S(1)}, f32[1,1,1,2,4,4,384]{6,5,0,4,3,2,1:T(4,128)S(1)}, u32[]{:S(2)}, u32[]{:S(2)}) collective-permute-start(f32[1,1,1,2,4,4,384]{6,5,0,4,3,2,1:T(4,128)S(1)} %get-tuple-element.70), channel_id=1, source_target_pairs={{0,2},{1,3},{2,4},{3,5},{4,6},{5,7},{6,0},{7,1},{8,10},{9,11},{10,... | collective-permute-start | bytes 147464 | tf_op jit(solution)/shard_map/ppermute | solution.py:93
  79.7 8.1 %collective-permute-start.8 = (f32[1,1,1,2,4,4,384]{6,5,0,4,3,2,1:T(4,128)S(1)}, f32[1,1,1,2,4,4,384]{6,5,0,4,3,2,1:T(4,128)S(1)}, u32[]{:S(2)}, u32[]{:S(2)}) collective-permute-start(f32[1,1,1,2,4,4,384]{6,5,0,4,3,2,1:T(4,128)S(1)} %get-tuple-element.69), channel_id=1, source_target_pairs={{0,3},{1,4},{2,5},{3,6},{4,7},{5,0},{6,1},{7,2},{8,11},{9,12},{10,... | collective-permute-start | bytes 147464 | tf_op jit(solution)/shard_map/ppermute | solution.py:93
  83.0 6.5 %collective-permute-start.9 = (f32[1,1,1,2,4,4,384]{6,5,0,4,3,2,1:T(4,128)S(1)}, f32[1,1,1,2,4,4,384]{6,5,0,4,3,2,1:T(4,128)S(1)}, u32[]{:S(2)}, u32[]{:S(2)}) collective-permute-start(f32[1,1,1,2,4,4,384]{6,5,0,4,3,2,1:T(4,128)S(1)} %get-tuple-element.68), channel_id=1, source_target_pairs={{0,4},{1,5},{2,6},{3,7},{4,0},{5,1},{6,2},{7,3},{8,12},{9,13},{10,... | collective-permute-start | bytes 147464 | tf_op jit(solution)/shard_map/ppermute | solution.py:93
  83.3 6.3 %collective-permute-start.10 = (f32[1,1,1,2,4,4,384]{6,5,0,4,3,2,1:T(4,128)S(1)}, f32[1,1,1,2,4,4,384]{6,5,0,4,3,2,1:T(4,128)S(1)}, u32[]{:S(2)}, u32[]{:S(2)}) collective-permute-start(f32[1,1,1,2,4,4,384]{6,5,0,4,3,2,1:T(4,128)S(1)} %get-tuple-element.67), channel_id=1, source_target_pairs={{0,5},{1,6},{2,7},{3,0},{4,1},{5,2},{6,3},{7,4},{8,13},{9,14},{10,... | collective-permute-start | bytes 147464 | tf_op jit(solution)/shard_map/ppermute | solution.py:93
  85.6 5.3 %collective-permute-start.11 = (f32[1,1,1,2,4,4,384]{6,5,0,4,3,2,1:T(4,128)S(1)}, f32[1,1,1,2,4,4,384]{6,5,0,4,3,2,1:T(4,128)S(1)}, u32[]{:S(2)}, u32[]{:S(2)}) collective-permute-start(f32[1,1,1,2,4,4,384]{6,5,0,4,3,2,1:T(4,128)S(1)} %get-tuple-element.66), channel_id=1, source_target_pairs={{0,6},{1,7},{2,0},{3,1},{4,2},{5,3},{6,4},{7,5},{8,14},{9,15},{10,... | collective-permute-start | bytes 147464 | tf_op jit(solution)/shard_map/ppermute | solution.py:93
  86.5 4.5 %collective-permute-start.12 = (f32[1,1,1,2,4,4,384]{6,5,0,4,3,2,1:T(4,128)S(1)}, f32[1,1,1,2,4,4,384]{6,5,0,4,3,2,1:T(4,128)S(1)}, u32[]{:S(2)}, u32[]{:S(2)}) collective-permute-start(f32[1,1,1,2,4,4,384]{6,5,0,4,3,2,1:T(4,128)S(1)} %get-tuple-element.65), channel_id=1, source_target_pairs={{0,7},{1,0},{2,1},{3,2},{4,3},{5,4},{6,5},{7,6},{8,15},{9,8},{10,9... | collective-permute-start | bytes 147464 | tf_op jit(solution)/shard_map/ppermute | solution.py:93
